TPU v7x, 512 devices: a whole 4x4x16 slice. The times are simulated.
512 devices in a mesh: dp: 32 (over z, x_hi), lon: 16 (over y, x_lo, core).
Axes of the slice: x: 4 (x_hi: 2, x_lo: 2; x = x_hi * 2 + x_lo), y: 4, z: 16, core: 2. Of those that a mesh axis runs over, the one named last changes fastest.
Arguments:
- fields: bfloat16 [32, 128, 48, 768], P('dp', 'lon'), may hold values from -6 to 6
- cotangent: bfloat16 [32, 128, 48, 768], P('dp', 'lon'), may hold values from -6 to 6
- first_weight: bfloat16 [2, 8, 96, 96], replicated, may hold values from -0.4375 to 0.4375
- second_weight: bfloat16 [2, 8, 96, 96], replicated, may hold values from -0.4375 to 0.4375
Outputs:
- layer_out: bfloat16 [32, 128, 48, 768], P('dp', 'lon')
- field_grad: bfloat16 [32, 128, 48, 768], P('dp', 'lon')
- first_grad: float32 [2, 8, 96, 96], replicated
- second_grad: float32 [2, 8, 96, 96], replicated
All inputs are finite; a program needn't handle non-finite values.
Results may differ from a plain program's by a relative error of at most 0.015.
Values may be sent and summed in bfloat16 or wider, within the bound.
A program may use at most 64 MiB of HBM per device.

v0:
```python
import math

import jax
import jax.numpy as jnp
from jax import lax
from jax.sharding import PartitionSpec as P

COEF = 0.7978845608028654
CUBIC = 0.044715


def gelu_value(inner):
    hyper = jnp.tanh(COEF * (inner + CUBIC * inner * inner * inner))
    return 0.5 * inner * (1.0 + hyper)


def gelu_slope(inner):
    hyper = jnp.tanh(COEF * (inner + CUBIC * inner * inner * inner))
    return 0.5 * (1.0 + hyper) + 0.5 * inner * (1.0 - hyper * hyper) * COEF * (
        1.0 + 3.0 * CUBIC * inner * inner
    )


def make_basis(length, count):
    cell_idx = jnp.arange(length, dtype=jnp.int32)
    mode_idx = jnp.arange(count, dtype=jnp.int32)
    product = cell_idx[:, None] * mode_idx[None, :] % length
    angle = product.astype(jnp.float32) * jnp.float32(2.0 * math.pi / length)
    return jnp.stack([jnp.cos(angle), -jnp.sin(angle)], axis=-1).astype(jnp.bfloat16)


def lat_apply(spec, table, lat_scale):
    return (
        jnp.einsum("kphc,phqj->kqjc", spec, table, preferred_element_type=jnp.float32) * lat_scale
    ).astype(jnp.bfloat16)


def forward_weight(weight):
    return jnp.stack([jnp.stack([weight[0], weight[1]]), jnp.stack([-weight[1], weight[0]])])


def adjoint_weight(weight):
    return jnp.stack([jnp.stack([weight[0], -weight[1]]), jnp.stack([weight[1], weight[0]])])


def block_product(spec, stacked):
    return jnp.einsum("kphbi,pqbij->kqhbj", spec, stacked, preferred_element_type=jnp.float32)


def block_adjoint(spec, stacked):
    return jnp.einsum("kphbj,pqbij->kqhbi", spec, stacked, preferred_element_type=jnp.float32)


def block_outer(left, right):
    pairs = jnp.einsum("kphbi,kqhbj->pqbij", left, right, preferred_element_type=jnp.float32)
    return jnp.stack([pairs[0, 0] + pairs[1, 1], pairs[0, 1] - pairs[1, 0]])


def on_device(fields, cotangent, first_weight, second_weight):
    cell_rows = fields[0]
    cot_rows = cotangent[0]
    lat_rows = cell_rows.shape[1]
    channels = cell_rows.shape[2]
    groups = first_weight.shape[1]
    group_width = first_weight.shape[2]
    lon_count = lax.axis_size("lon")
    total_cells = cell_rows.shape[0] * lon_count
    dft_basis = make_basis(total_cells, total_cells // 2)
    lat_basis = make_basis(lat_rows, lat_rows)
    cos_tab = lat_basis[:, :, 0]
    sin_tab = lat_basis[:, :, 1]
    lat_fwd_table = jnp.stack(
        [jnp.stack([cos_tab, sin_tab], axis=1), jnp.stack([-sin_tab, cos_tab], axis=1)], axis=0
    )
    lat_inv_table = jnp.stack(
        [jnp.stack([cos_tab.T, -sin_tab.T], axis=1), jnp.stack([sin_tab.T, cos_tab.T], axis=1)],
        axis=0,
    )
    norm_scale = 1.0 / math.sqrt(total_cells)
    lat_scale = 1.0 / math.sqrt(lat_rows)
    local_modes = cell_rows.shape[0] // 2
    mode_idx = lax.axis_index("lon") * local_modes + jnp.arange(local_modes, dtype=jnp.int32)
    mode_weight = jnp.where(mode_idx == 0, 1.0, 2.0).astype(jnp.bfloat16)[:, None, None, None]
    first_fwd = forward_weight(first_weight)
    second_fwd = forward_weight(second_weight)
    first_adj = adjoint_weight(first_weight)
    second_adj = adjoint_weight(second_weight)

    def local_dft(all_lines):
        return (
            jnp.einsum("whc,wkp->kphc", all_lines, dft_basis, preferred_element_type=jnp.float32)
            * norm_scale
        ).astype(jnp.bfloat16)

    def local_idft(all_modes):
        return (
            jnp.einsum("kphc,wkp->whc", all_modes, dft_basis, preferred_element_type=jnp.float32)
            * norm_scale
        ).astype(jnp.bfloat16)

    def lines_to_modes(all_lines):
        return lax.all_to_all(local_dft(all_lines), "lon", split_axis=0, concat_axis=3, tiled=True)

    def modes_to_lines(all_modes):
        return lax.all_to_all(local_idft(all_modes), "lon", split_axis=0, concat_axis=2, tiled=True)

    def to_spectrum(grid_rows):
        return lines_to_modes(
            lax.all_to_all(grid_rows, "lon", split_axis=2, concat_axis=0, tiled=True)
        )

    def to_cells(spec_rows):
        return modes_to_lines(
            lax.all_to_all(spec_rows, "lon", split_axis=3, concat_axis=0, tiled=True)
        )

    def split_groups(spec_rows):
        return spec_rows.reshape(local_modes, 2, lat_rows, groups, group_width)

    def join_groups(spec_rows):
        return spec_rows.astype(jnp.bfloat16).reshape(local_modes, 2, lat_rows, channels)

    lon_spec = to_spectrum(cell_rows)
    spectrum = split_groups(lat_apply(lon_spec, lat_fwd_table, lat_scale))
    inner = block_product(spectrum, first_fwd)
    act = gelu_value(inner).astype(jnp.bfloat16)
    mixed = join_groups(block_product(act, second_fwd)) * mode_weight
    mixed_lon = lat_apply(mixed, lat_inv_table, lat_scale)
    wave = to_cells(mixed_lon)
    dual_lon = to_spectrum(cot_rows)
    dual = split_groups(lat_apply(dual_lon, lat_fwd_table, lat_scale) * mode_weight)
    back = block_adjoint(dual, second_adj)
    pre = (back * gelu_slope(inner)).astype(jnp.bfloat16)
    back_spec = join_groups(block_adjoint(pre, first_adj))
    back_lon = lat_apply(back_spec, lat_inv_table, lat_scale)
    pull = to_cells(back_lon)
    layer_out = (cell_rows.astype(jnp.float32) + wave.astype(jnp.float32)).astype(jnp.bfloat16)
    field_grad = (cot_rows.astype(jnp.float32) + pull.astype(jnp.float32)).astype(jnp.bfloat16)
    sample_count = lax.axis_size("dp")
    second_term = block_outer(act, dual) / sample_count
    first_term = block_outer(spectrum, pre) / sample_count
    first_grad, second_grad = lax.psum((first_term, second_term), ("dp", "lon"))
    return (layer_out[None], field_grad[None], first_grad, second_grad)


def solution(mesh):
    placed = (P("dp", "lon", None, None), P("dp", "lon", None, None), P(), P())
    return jax.shard_map(
        on_device,
        mesh=mesh,
        in_specs=placed,
        out_specs=(P("dp", "lon", None, None), P("dp", "lon", None, None), P(), P()),
        check_vma=False,
    )
```

profile of v0, /device:TPU:1, one launch (start us, length us, event | category | flops | bytes accessed | tf_op | source)
XLA Modules:
  0.0 643.1 jit_solution(1187848861176454927)
XLA Ops:
  9.3 3.1 reshape.309
  12.4 11.0 %all-to-all-start = ((bf16[16,2,9216]{2,1,0:T(2,128)(2,1)}), bf16[16,2,9216]{2,1,0:T(2,128)(2,1)}, u32[]{:S(2)}, u32[]{:S(2)}) async-start(bf16[16,2,9216]{2,1,0:T(2,128)(2,1)} %reshape.309), calls=%async_computation | async-start | bytes 1179648 | tf_op jit(solution)/shard_map/all_to_all | solution.py:109
  24.6 3.1 reshape.317
  30.0 4.0 all-to-all-done
  34.1 5.2 all-to-all-start.4
  40.8 2.4 reshape.310
  47.2 3.1 reshape.311
  50.3 6.1 all-to-all-start.1
  65.1 3.1 reshape.319
  68.2 5.9 all-to-all-start.5
  76.8 2.4 reshape.312
  84.7 2.4 reshape.320
  89.4 3.1 reshape.288
  101.2 3.1 reshape.321
  104.3 4.6 all-to-all-start.6
  115.7 4.1 reshape.313
  121.3 5.8 all-to-all-start.2
  135.5 3.1 reshape.323
  138.6 5.7 all-to-all-start.7
  151.3 3.1 reshape.315
  154.4 451.1 %all-reduce.3.cloned.1.call-done = (f32[2,8,96,96]{2,3,1,0:T(8,128)}, f32[2,8,96,96]{2,3,1,0:T(8,128)}) async-done(((f32[2,8,96,96]{2,3,1,0:T(8,128)}, f32[2,8,96,96]{2,3,1,0:T(8,128)}), (f32[2,8,96,96]{2,3,1,0:T(8,128)}, f32[2,8,96,96]{2,3,1,0:T(8,128)})) %all-reduce.3.cloned.1.call-update) | async-done | bytes 1179664 | tf_op jit(solution)/shard_map/psum | solution.py:142
  609.0 7.4 %all-to-all-start.3 = ((bf16[16,2,9216]{2,1,0:T(2,128)(2,1)}), bf16[16,2,9216]{2,1,0:T(2,128)(2,1)}, u32[]{:S(2)}, u32[]{:S(2)}) async-start(bf16[16,2,9216]{2,1,0:T(2,128)(2,1)} %reshape.315), calls=%async_computation.3 | async-start | bytes 1179648 | tf_op jit(solution)/shard_map/all_to_all | solution.py:105
  616.4 2.4 reshape.324
  626.9 2.4 reshape.316
  (147 shorter events, 80.4 us)
Async XLA Ops:
  12.3 11.0 %copy-start = (bf16[1,8,48,768]{3,2,1,0:T(8,128)(2,1)S(1)}, bf16[1,8,48,768]{3,2,1,0:T(8,128)(2,1)}, u32[]{:S(2)}) copy-start(bf16[1,8,48,768]{3,2,1,0:T(8,128)(2,1)} %param.5) | copy-start | bytes 1769476
  12.4 21.7 %all-to-all-start = ((bf16[16,2,9216]{2,1,0:T(2,128)(2,1)}), bf16[16,2,9216]{2,1,0:T(2,128)(2,1)}, u32[]{:S(2)}, u32[]{:S(2)}) async-start(bf16[16,2,9216]{2,1,0:T(2,128)(2,1)} %reshape.309), calls=%async_computation | async-start | bytes 1179648 | tf_op jit(solution)/shard_map/all_to_all | solution.py:109
  24.6 15.4 %copy-start.21 = (bf16[2,8,96,96]{3,2,1,0:T(8,128)(2,1)S(1)}, bf16[2,8,96,96]{3,2,1,0:T(8,128)(2,1)}, u32[]{:S(2)}) copy-start(bf16[2,8,96,96]{3,2,1,0:T(8,128)(2,1)} %param.6) | copy-start | bytes 884740
  34.1 16.2 %all-to-all-start.4 = ((bf16[16,2,9216]{2,1,0:T(2,128)(2,1)}), bf16[16,2,9216]{2,1,0:T(2,128)(2,1)}, u32[]{:S(2)}, u32[]{:S(2)}) async-start(bf16[16,2,9216]{2,1,0:T(2,128)(2,1)} %reshape.317), calls=%async_computation.4 | async-start | bytes 1179648 | tf_op jit(solution)/shard_map/all_to_all | solution.py:109
  47.2 9.3 %copy-start.29 = (bf16[48,1,48]{2,0,1:T(8,128)(2,1)S(1)}, bf16[48,1,48]{2,0,1:T(8,128)(2,1)}, u32[]{:S(2)}) copy-start(bf16[48,1,48]{2,0,1:T(8,128)(2,1)} %get-tuple-element.48) | copy-start | bytes 13828
  47.2 9.3 %copy-start.30 = (bf16[48,1,48]{2,0,1:T(8,128)(2,1)S(1)}, bf16[48,1,48]{2,0,1:T(8,128)(2,1)}, u32[]{:S(2)}) copy-start(bf16[48,1,48]{2,0,1:T(8,128)(2,1)} %get-tuple-element.49) | copy-start | bytes 13828
  47.2 9.3 %copy-start.31 = (bf16[48,1,48]{2,0,1:T(8,128)(2,1)S(1)}, bf16[48,1,48]{2,0,1:T(8,128)(2,1)}, u32[]{:S(2)}) copy-start(bf16[48,1,48]{2,0,1:T(8,128)(2,1)} %fusion.91) | copy-start | bytes 13828
  47.2 9.9 %copy-start.22 = (bf16[2,8,96,96]{3,2,1,0:T(8,128)(2,1)S(1)}, bf16[2,8,96,96]{3,2,1,0:T(8,128)(2,1)}, u32[]{:S(2)}) copy-start(bf16[2,8,96,96]{3,2,1,0:T(8,128)(2,1)} %param.7) | copy-start | bytes 884740
  50.3 17.9 %all-to-all-start.1 = ((bf16[16,2,9216]{2,1,0:T(2,128)(2,1)}), bf16[16,2,9216]{2,1,0:T(2,128)(2,1)}, u32[]{:S(2)}, u32[]{:S(2)}) async-start(bf16[16,2,9216]{2,1,0:T(2,128)(2,1)} %reshape.311), calls=%async_computation.1 | async-start | bytes 1179648 | tf_op jit(solution)/shard_map/all_to_all | solution.py:102
  65.1 9.5 %copy-start.8 = (bf16[1,8,96,96]{3,2,0,1:T(8,128)(2,1)S(1)}, bf16[1,8,96,96]{3,2,0,1:T(8,128)(2,1)}, u32[]{:S(2)}) copy-start(bf16[1,8,96,96]{3,2,0,1:T(8,128)(2,1)} %get-tuple-element.26) | copy-start | bytes 442372
  65.1 9.5 %copy-start.9 = (bf16[1,8,96,96]{3,2,0,1:T(8,128)(2,1)S(1)}, bf16[1,8,96,96]{3,2,0,1:T(8,128)(2,1)}, u32[]{:S(2)}) copy-start(bf16[1,8,96,96]{3,2,0,1:T(8,128)(2,1)} %get-tuple-element.27) | copy-start | bytes 442372
  65.1 9.5 %copy-start.10 = (bf16[1,8,96,96]{3,2,0,1:T(8,128)(2,1)S(1)}, bf16[1,8,96,96]{3,2,0,1:T(8,128)(2,1)}, u32[]{:S(2)}) copy-start(bf16[1,8,96,96]{3,2,0,1:T(8,128)(2,1)} %get-tuple-element.28) | copy-start | bytes 442372
  68.2 7.5 %copy-start.11 = (bf16[1,8,96,96]{3,2,0,1:T(8,128)(2,1)S(1)}, bf16[1,8,96,96]{3,2,0,1:T(8,128)(2,1)}, u32[]{:S(2)}) copy-start(bf16[1,8,96,96]{3,2,0,1:T(8,128)(2,1)} %get-tuple-element.31) | copy-start | bytes 442372
  68.2 7.5 %copy-start.12 = (bf16[1,8,96,96]{3,2,0,1:T(8,128)(2,1)S(1)}, bf16[1,8,96,96]{3,2,0,1:T(8,128)(2,1)}, u32[]{:S(2)}) copy-start(bf16[1,8,96,96]{3,2,0,1:T(8,128)(2,1)} %get-tuple-element.32) | copy-start | bytes 442372
  68.2 7.5 %copy-start.13 = (bf16[1,8,96,96]{3,2,0,1:T(8,128)(2,1)S(1)}, bf16[1,8,96,96]{3,2,0,1:T(8,128)(2,1)}, u32[]{:S(2)}) copy-start(bf16[1,8,96,96]{3,2,0,1:T(8,128)(2,1)} %get-tuple-element.33) | copy-start | bytes 442372
  68.2 16.5 %all-to-all-start.5 = ((bf16[16,2,9216]{2,1,0:T(2,128)(2,1)}), bf16[16,2,9216]{2,1,0:T(2,128)(2,1)}, u32[]{:S(2)}, u32[]{:S(2)}) async-start(bf16[16,2,9216]{2,1,0:T(2,128)(2,1)} %reshape.319), calls=%async_computation.5 | async-start | bytes 1179648 | tf_op jit(solution)/shard_map/all_to_all | solution.py:102
  89.4 3.2 copy-start.28
  89.4 3.2 copy-start.32
  101.2 7.6 %copy-start.3 = (bf16[2,8,96,96]{3,2,0,1:T(8,128)(2,1)S(1)}, bf16[2,8,96,96]{3,2,0,1:T(8,128)(2,1)}, u32[]{:S(2)}) copy-start(bf16[2,8,96,96]{3,2,0,1:T(8,128)(2,1)} %copy-done.2) | copy-start | bytes 884740
  104.3 17.0 %all-to-all-start.6 = ((bf16[16,2,9216]{2,1,0:T(2,128)(2,1)}), bf16[16,2,9216]{2,1,0:T(2,128)(2,1)S(1)}, u32[]{:S(2)}, u32[]{:S(2)}) async-start(bf16[16,2,9216]{2,1,0:T(2,128)(2,1)} %reshape.321), calls=%async_computation.6 | async-start | bytes 1179648 | tf_op jit(solution)/shard_map/all_to_all | solution.py:114
  121.3 17.3 %all-to-all-start.2 = ((bf16[16,2,9216]{2,1,0:T(2,128)(2,1)}), bf16[16,2,9216]{2,1,0:T(2,128)(2,1)}, u32[]{:S(2)}, u32[]{:S(2)}) async-start(bf16[16,2,9216]{2,1,0:T(2,128)(2,1)} %reshape.313), calls=%async_computation.2 | async-start | bytes 1179648 | tf_op jit(solution)/shard_map/all_to_all | solution.py:114
  127.1 478.4 %all-reduce.3.cloned.1.call-start = ((), (), s32[]{:S(2)}) async-start(), calls=%async_computation.8 | async-start | bytes 3145728 | tf_op jit(solution)/shard_map/psum | solution.py:142
  138.6 470.4 %all-to-all-start.7 = ((bf16[16,2,9216]{2,1,0:T(2,128)(2,1)}), bf16[16,2,9216]{2,1,0:T(2,128)(2,1)}, u32[]{:S(2)}, u32[]{:S(2)}) async-start(bf16[16,2,9216]{2,1,0:T(2,128)(2,1)} %reshape.323), calls=%async_computation.7 | async-start | bytes 1179648 | tf_op jit(solution)/shard_map/all_to_all | solution.py:105
  609.0 17.9 %all-to-all-start.3 = ((bf16[16,2,9216]{2,1,0:T(2,128)(2,1)}), bf16[16,2,9216]{2,1,0:T(2,128)(2,1)}, u32[]{:S(2)}, u32[]{:S(2)}) async-start(bf16[16,2,9216]{2,1,0:T(2,128)(2,1)} %reshape.315), calls=%async_computation.3 | async-start | bytes 1179648 | tf_op jit(solution)/shard_map/all_to_all | solution.py:105
  (18 other events, 26.0 us)
Sparse Core Ops, SparseCore 0:
  133.9 471.5 all-reduce.2
where the time goes:
time: 651 us; the launch traced here: 643 us
  waiting for transfers between devices  458 us (70%)
  local copies, waits for them, and re-layouts  88.8 us (14%)
  starting transfers between devices  51.6 us (8%)
  other arithmetic  17.4 us (3%)
  between operations  15 us (2%)
  matrix products  12.2 us (2%)
    psum x1, waiting for transfers between devices, on_device(): first_grad, second_grad = lax.psum((first_term, second_term), ('dp', 'lon'))  451 us
    unnamed x90, local copies, waits for them, and re-layouts  52.7 us
    all_to_all x2, starting transfers between devices, to_spectrum(): lax.all_to_all(grid_rows, 'lon', split_axis=2, concat_axis=0, tiled=True)  16.1 us
    all_to_all x2, starting transfers between devices, modes_to_lines(): lax.all_to_all(local_idft(all_modes), 'lon', split_axis=0, concat_axis=2,...  13.1 us
  transfers between devices with their start and end apart: 9, of which 4 were waited for; matrix products, arithmetic and copies ran while one was open for 13% of the time, Pallas kernels for 0%

commit v1 on v0

v1 whole, which is shorter than its diff:
```python
import math

import jax
import jax.numpy as jnp
import ml_dtypes
import numpy as np
from jax import lax
from jax.experimental import pallas as pl
from jax.experimental.pallas import tpu as pltpu
from jax.sharding import PartitionSpec as P

COEF = 0.7978845608028654
CUBIC = 0.044715

SAMPLES = 32
CELLS = 128
LAT = 48
MODES = 64
CHANNELS = 768
GROUPS = 8
WIDTH = 96

LON = 16
ROWS = CELLS // LON
HALF = CHANNELS // 2
PAIRS = LAT // 2
OWN = PAIRS // (LON // 2)
TILE = 2 * ROWS
LINES = OWN * 2 * MODES
TILES = 9
SCALE = 1.0 / math.sqrt(CELLS * LAT)
MESH = pl.DeviceIdType.MESH
BF16 = jnp.bfloat16
F32 = jnp.float32


def make_basis(length, count):
    product = np.arange(length)[:, None] * np.arange(count)[None, :] % length
    angle = product.astype(np.float32) * np.float32(2.0 * math.pi / length)
    table = np.stack([np.cos(angle), -np.sin(angle)], axis=-1)
    return table.astype(ml_dtypes.bfloat16).astype(np.float32)


def lat_matrix():
    table = make_basis(LAT, LAT)
    half = np.zeros((PAIRS, 2, LAT), np.float32)
    half[0, 0] = table[:, 0, 0]
    half[0, 1] = table[:, PAIRS, 0]
    for j in range(1, PAIRS):
        half[j, 0] = table[:, j, 0]
        half[j, 1] = table[:, j, 1]
    full = np.einsum("pah,wv->pawvh", half, np.eye(ROWS, dtype=np.float32))
    return full.reshape(PAIRS * 2 * ROWS, ROWS * LAT)


def lon_matrix(special, weighted):
    table = make_basis(CELLS, MODES)
    cos, sin = table[:, :, 0].T, table[:, :, 1].T
    if weighted:
        factor = np.where(np.arange(MODES) == 0, 1.0, 2.0).astype(np.float32)[:, None]
        cos, sin = cos * factor, sin * factor
    zero = np.zeros_like(cos)
    if special:
        from_real = [cos, sin, zero, zero]
        from_imag = [zero, zero, cos, sin]
    else:
        from_real = [cos, sin, cos, sin]
        from_imag = [-sin, cos, sin, -cos]
    both = np.stack([np.concatenate(from_real), np.concatenate(from_imag)], axis=1)
    both = both.reshape(4 * MODES, 2, LON, ROWS).transpose(0, 2, 1, 3)
    return both.reshape(4 * MODES, 2 * CELLS)


def lon_matrices():
    found = []
    for special in (False, True):
        plain, weighted = lon_matrix(special, False), lon_matrix(special, True)
        found += [plain, weighted, plain.T, weighted.T]
    return np.stack(found)


def matmul(left, right):
    return jnp.dot(left, right, preferred_element_type=F32)


def contract(left, right, axis):
    return lax.dot_general(
        left, right, (((axis,), (axis,)), ((), ())), preferred_element_type=F32
    )


def kernel(
    x_hbm, y_hbm, w1_hbm, w2_hbm, lon_hbm, latf_hbm, lati_hbm,
    outx_hbm, outy_hbm, grad1_hbm, grad2_hbm,
    xv, yv, w1v, w2v, lonv, latf, lati,
    send_x, send_y, recv_x, recv_y, back_x, back_y, home_x, home_y,
    wide1, wide2, place, spec, dual, act, pre, slope, mixed,
    square, grads, part1, own1, part2, own3, final, strip, grad1, grad2,
    load_sem, store_sem, self_sem, out_sem, in_sem,
    sum_out, sum_in, dp_out, dp_in, cast_out, cast_in, gather_out, gather_in,
):
    dp_count = lax.axis_size("dp")
    me, dp = lax.axis_index("lon"), lax.axis_index("dp")

    def half_of(s):
        return lax.rem(s // 2, 2)

    def slot_of(s):
        return (s // 4) * 2 + lax.rem(s, 2)

    def device_of(e, u):
        return (e // 2) * 4 + u * 2 + lax.rem(e, 2)

    u, e = half_of(me), slot_of(me)
    first = jnp.where(e == 0, 4, 0)

    loads = [
        pltpu.make_async_copy(x_hbm, xv, load_sem.at[0]),
        pltpu.make_async_copy(latf_hbm, latf, load_sem.at[1]),
        pltpu.make_async_copy(y_hbm, yv, load_sem.at[2]),
        pltpu.make_async_copy(w1_hbm, w1v, load_sem.at[3]),
        pltpu.make_async_copy(w2_hbm, w2v, load_sem.at[4]),
        pltpu.make_async_copy(lon_hbm.at[pl.ds(0, 4)], lonv.at[pl.ds(0, 4)], load_sem.at[5]),
        pltpu.make_async_copy(lon_hbm.at[pl.ds(first, 4)], lonv.at[pl.ds(4, 4)], load_sem.at[6]),
        pltpu.make_async_copy(lati_hbm, lati, load_sem.at[7]),
    ]
    for load in loads:
        load.start()

    barrier = pltpu.get_barrier_semaphore()

    @pl.loop(1, LON)
    def _(i):
        pl.semaphore_signal(
            barrier, inc=1, device_id=(dp, lax.rem(me + i, LON)), device_id_type=MESH
        )

    @pl.loop(1, dp_count)
    def _(i):
        pl.semaphore_signal(
            barrier, inc=1, device_id=(lax.rem(dp + i, dp_count), me), device_id_type=MESH
        )

    def lat_forward(rows, out):
        for n in range(3):
            lanes = slice(256 * n, 256 * n + 256)
            got = matmul(latf[...], rows[:, lanes]).astype(BF16)
            out[:, :, lanes] = got.reshape(PAIRS, TILE, 256)

    def block_of(buf, s):
        lanes = pl.ds(pl.multiple_of(half_of(s) * HALF, 128), HALF)
        return buf.at[pl.ds(slot_of(s) * OWN, OWN), :, lanes]

    def to_mixer(stage, src, dst, i):
        s = lax.rem(me + i, LON)
        return pltpu.make_async_remote_copy(
            src_ref=block_of(src, s),
            dst_ref=dst.at[:, me],
            send_sem=out_sem.at[stage, i],
            recv_sem=in_sem.at[stage, me],
            device_id=(dp, s),
            device_id_type=MESH,
        )

    def to_cells(stage, src, dst, i):
        s = lax.rem(me + i, LON)
        return pltpu.make_async_remote_copy(
            src_ref=src.at[:, s],
            dst_ref=block_of(dst, me),
            send_sem=out_sem.at[stage, i],
            recv_sem=in_sem.at[stage, me],
            device_id=(dp, s),
            device_id_type=MESH,
        )

    def start_all(make, stage, src, dst):
        @pl.loop(1, LON)
        def _(i):
            make(stage, src, dst, i).start()

    def arrived(stage, buf):
        @pl.loop(1, LON)
        def _(i):
            s = lax.rem(me + i, LON)
            if stage < 2:
                spot = buf.at[:, s]
            else:
                spot = block_of(buf, s)
            pltpu.make_async_remote_copy(
                src_ref=spot,
                dst_ref=spot,
                send_sem=out_sem.at[stage, i],
                recv_sem=in_sem.at[stage, s],
                device_id=(dp, s),
                device_id_type=MESH,
            ).wait_recv()

    def keep_forward(src, dst, n):
        return pltpu.make_async_copy(block_of(src, me), dst.at[:, me], self_sem.at[n])

    def keep_back(src, dst, n):
        return pltpu.make_async_copy(src.at[:, me], block_of(dst, me), self_sem.at[n])

    loads[0].wait()
    loads[1].wait()
    lat_forward(xv, send_x)
    pl.semaphore_wait(barrier, LON - 1 + dp_count - 1)
    start_all(to_mixer, 0, send_x, recv_x)
    keep_x = keep_forward(send_x, recv_x, 0)
    keep_x.start()
    loads[2].wait()
    lat_forward(yv, send_y)
    start_all(to_mixer, 1, send_y, recv_y)
    keep_y = keep_forward(send_y, recv_y, 1)
    keep_y.start()

    def widen(weight, wide):
        for p in range(2):
            for g in range(4):
                own = slice(WIDTH * g, WIDTH * g + WIDTH)
                place[p, own, own] = weight[p, 4 * u + g].astype(F32)
        real, imag = place[0].astype(BF16), place[1].astype(BF16)
        wide[:HALF, :HALF] = real
        wide[HALF:, HALF:] = real
        wide[:HALF, HALF:] = imag
        wide[HALF:, :HALF] = -imag

    place[...] = jnp.zeros_like(place)
    for load in loads[3:]:
        load.wait()
    widen(w1v, wide1)
    widen(w2v, wide2)

    def lon_forward(buf, kind, out):
        for p in range(OWN):
            table = lonv[kind + (4 if p == 0 else 0)]
            got = matmul(table, buf[p].reshape(2 * CELLS, HALF))
            got = (got * SCALE).astype(BF16)
            for x in range(2):
                rows = slice((2 * p + x) * MODES, (2 * p + x + 1) * MODES)
                out[rows, :HALF] = got[2 * x * MODES : (2 * x + 1) * MODES]
                out[rows, HALF:] = got[(2 * x + 1) * MODES : (2 * x + 2) * MODES]

    def store_mixed(got, part):
        for p in range(OWN):
            for x in range(2):
                rows = slice((2 * p + x) * MODES, (2 * p + x + 1) * MODES)
                to = slice((2 * x + part) * MODES, (2 * x + part + 1) * MODES)
                mixed[p, to, :] = got[rows]

    def lon_inverse(kind, out):
        for p in range(OWN):
            table = lonv[kind + (4 if p == 0 else 0)]
            got = matmul(table, mixed[p]).astype(BF16)
            out[p] = got.reshape(LON, TILE, HALF)

    keep_x.wait()
    arrived(0, recv_x)
    lon_forward(recv_x, 0, spec)
    for part in range(2):
        lanes = slice(HALF * part, HALF * part + HALF)
        inner = matmul(spec[...], wide1[:, lanes])
        hyper = jnp.tanh(COEF * (inner + CUBIC * inner * inner * inner))
        act[:, lanes] = (0.5 * inner * (1.0 + hyper)).astype(BF16)
        slope[:, lanes] = 0.5 * (1.0 + hyper) + 0.5 * inner * (1.0 - hyper * hyper) * COEF * (
            1.0 + 3.0 * CUBIC * inner * inner
        )
    for part in range(2):
        lanes = slice(HALF * part, HALF * part + HALF)
        store_mixed(matmul(act[...], wide2[:, lanes]).astype(BF16), part)
    lon_inverse(3, back_x)
    start_all(to_cells, 2, back_x, home_x)
    keep_x = keep_back(back_x, home_x, 2)
    keep_x.start()

    def outer(left, right, n):
        for m in range(6):
            lanes = slice(128 * m, 128 * m + 128)
            square[lanes, :] = contract(left[:, lanes], right[...], 0)
        lane = lax.broadcasted_iota(jnp.int32, (WIDTH, 128), 1)
        for b in range(3):
            low = slice(128 * b, 128 * b + 128)
            high = slice(HALF + 128 * b, HALF + 128 * b + 128)
            sums, gaps = [], []
            for g in (b, b + 1):
                top = slice(WIDTH * g, WIDTH * g + WIDTH)
                bottom = slice(HALF + WIDTH * g, HALF + WIDTH * g + WIDTH)
                sums.append(square[top, low] + square[bottom, high])
                gaps.append(square[top, high] - square[bottom, low])
            mine = lane < WIDTH - 32 * b
            grads[n, :, low] = jnp.where(mine, sums[0], sums[1]).astype(BF16)
            grads[n + 1, :, low] = jnp.where(mine, gaps[0], gaps[1]).astype(BF16)

    keep_y.wait()
    arrived(1, recv_y)
    lon_forward(recv_y, 1, dual)
    for part in range(2):
        rows = slice(HALF * part, HALF * part + HALF)
        back = contract(dual[...], wide2[rows, :], 1)
        pre[:, rows] = (back * slope[:, rows]).astype(BF16)
    outer(spec, pre, 0)
    outer(act, dual, 2)

    def share(k):
        return grads.at[k // 2, pl.ds(pl.multiple_of(lax.rem(k, 2) * 48, 16), 48), :]

    @pl.loop(1, 8)
    def _(i):
        k = lax.rem(e + i, 8)
        pltpu.make_async_remote_copy(
            src_ref=share(k),
            dst_ref=part1.at[e],
            send_sem=sum_out.at[i],
            recv_sem=sum_in.at[e],
            device_id=(dp, device_of(k, u)),
            device_id_type=MESH,
        ).start()

    for part in range(2):
        rows = slice(HALF * part, HALF * part + HALF)
        store_mixed(contract(pre[...], wide1[rows, :], 1).astype(BF16), part)
    lon_inverse(2, back_y)
    start_all(to_cells, 3, back_y, home_y)
    keep_y = keep_back(back_y, home_y, 3)
    keep_y.start()

    part1[e] = share(e)[...]

    @pl.loop(1, 8)
    def _(i):
        k = lax.rem(e + i, 8)
        pltpu.make_async_remote_copy(
            src_ref=part1.at[k],
            dst_ref=part1.at[k],
            send_sem=sum_out.at[i],
            recv_sem=sum_in.at[k],
            device_id=(dp, device_of(k, u)),
            device_id_type=MESH,
        ).wait_recv()

    total = part1[0].astype(F32)
    for k in range(1, 8):
        total = total + part1[k].astype(F32)
    total = total.astype(BF16)
    for t in range(TILES):
        a, b = t // 3, t % 3
        own1[t] = total[16 * a : 16 * a + 16, 128 * b : 128 * b + 128]

    def reducer(t):
        return (dp_count * t) // TILES

    def to_reducer(t):
        return pltpu.make_async_remote_copy(
            src_ref=own1.at[t],
            dst_ref=part2.at[dp],
            send_sem=dp_out.at[t],
            recv_sem=dp_in.at[dp],
            device_id=(reducer(t), me),
            device_id_type=MESH,
        )

    @pl.loop(0, TILES)
    def _(t):
        @pl.when(dp != reducer(t))
        def _():
            to_reducer(t).start()

    def finish_cells(rows, home, out, n):
        for c in range(3):
            lanes = slice(256 * c, 256 * c + 256)
            got = matmul(lati[...], home[:, :, lanes].reshape(LAT * ROWS, 256))
            got = (got * SCALE).astype(BF16).astype(F32) + rows[:, lanes].astype(F32)
            rows[:, lanes] = got.astype(BF16)
        return pltpu.make_async_copy(rows, out, store_sem.at[n])

    keep_x.wait()
    arrived(2, home_x)
    store_x = finish_cells(xv, home_x, outx_hbm, 0)
    store_x.start()

    mine = ((TILES * dp) + TILES - 1) // dp_count
    reduces = reducer(mine) == dp

    def to_all(i):
        d = lax.rem(dp + i, dp_count)
        return pltpu.make_async_remote_copy(
            src_ref=own3.at[mine],
            dst_ref=own3.at[mine],
            send_sem=cast_out.at[i],
            recv_sem=cast_in.at[mine],
            device_id=(d, me),
            device_id_type=MESH,
        )

    @pl.when(reduces)
    def _():
        part2[dp] = own1[mine]

        @pl.loop(1, dp_count)
        def _(i):
            d = lax.rem(dp + i, dp_count)
            pltpu.make_async_remote_copy(
                src_ref=part2.at[d],
                dst_ref=part2.at[d],
                send_sem=dp_out.at[0],
                recv_sem=dp_in.at[d],
                device_id=(d, me),
                device_id_type=MESH,
            ).wait_recv()

        whole = part2[0].astype(F32)
        for d in range(1, dp_count):
            whole = whole + part2[d].astype(F32)
        own3[mine] = (whole * (1.0 / SAMPLES)).astype(BF16)

        @pl.loop(1, dp_count)
        def _(i):
            to_all(i).start()

    @pl.loop(0, TILES)
    def _(t):
        @pl.when(dp != reducer(t))
        def _():
            pltpu.make_async_remote_copy(
                src_ref=own3.at[t],
                dst_ref=own3.at[t],
                send_sem=cast_out.at[0],
                recv_sem=cast_in.at[t],
                device_id=(reducer(t), me),
                device_id_type=MESH,
            ).wait_recv()

    def to_group(i):
        return pltpu.make_async_remote_copy(
            src_ref=own3,
            dst_ref=final.at[me],
            send_sem=gather_out.at[i],
            recv_sem=gather_in.at[me],
            device_id=(dp, lax.rem(me + i, LON)),
            device_id_type=MESH,
        )

    @pl.loop(1, LON)
    def _(i):
        to_group(i).start()

    final[me] = own3[...]

    keep_y.wait()
    arrived(3, home_y)
    store_y = finish_cells(yv, home_y, outy_hbm, 1)
    store_y.start()

    @pl.loop(1, LON)
    def _(i):
        s = lax.rem(me + i, LON)
        pltpu.make_async_remote_copy(
            src_ref=final.at[s],
            dst_ref=final.at[s],
            send_sem=gather_out.at[i],
            recv_sem=gather_in.at[s],
            device_id=(dp, s),
            device_id_type=MESH,
        ).wait_recv()

    for q in range(4):
        out = (grad1, grad2)[q // 2]
        for v in range(2):
            for t in range(2 * TILES):
                a, b = t // 3, t % 3
                tile = final[4 * q + 2 * v + a // 3, 3 * (a % 3) + b]
                strip[16 * a : 16 * a + 16, 128 * b : 128 * b + 128] = tile.astype(F32)
            for g in range(4):
                out[q % 2, 4 * v + g] = strip[:, WIDTH * g : WIDTH * g + WIDTH]

    stores = [
        pltpu.make_async_copy(grad1, grad1_hbm, store_sem.at[2]),
        pltpu.make_async_copy(grad2, grad2_hbm, store_sem.at[3]),
    ]
    for store in stores:
        store.start()

    @pl.loop(1, LON)
    def _(i):
        to_mixer(0, send_x, recv_x, i).wait_send()
        to_mixer(1, send_y, recv_y, i).wait_send()
        to_cells(2, back_x, home_x, i).wait_send()
        to_cells(3, back_y, home_y, i).wait_send()
        to_group(i).wait_send()

    @pl.loop(1, 8)
    def _(i):
        k = lax.rem(e + i, 8)
        pltpu.make_async_remote_copy(
            src_ref=share(k),
            dst_ref=part1.at[e],
            send_sem=sum_out.at[i],
            recv_sem=sum_in.at[e],
            device_id=(dp, device_of(k, u)),
            device_id_type=MESH,
        ).wait_send()

    @pl.loop(0, TILES)
    def _(t):
        @pl.when(dp != reducer(t))
        def _():
            to_reducer(t).wait_send()

    @pl.when(reduces)
    def _():
        @pl.loop(1, dp_count)
        def _(i):
            to_all(i).wait_send()

    for store in [store_x, store_y, *stores]:
        store.wait()


def on_device(fields, cotangent, first_weight, second_weight):
    dp_count = lax.axis_size("dp")
    rows = ROWS * LAT
    lon = jnp.asarray(lon_matrices(), BF16)
    lat = lat_matrix()
    lat_fwd, lat_inv = jnp.asarray(lat, BF16), jnp.asarray(lat.T.copy(), BF16)
    weight_shape = (2, GROUPS, WIDTH, WIDTH)
    any_spec = pl.BlockSpec(memory_space=pl.ANY)
    dma = pltpu.SemaphoreType.DMA
    cells = pltpu.VMEM((rows, CHANNELS), BF16)
    pairs = pltpu.VMEM((PAIRS, TILE, CHANNELS), BF16)
    lines = pltpu.VMEM((LINES, CHANNELS), BF16)
    blocks = pltpu.VMEM((OWN, LON, TILE, HALF), BF16)
    side = 4 * MODES
    wave, pull, grad1, grad2 = pl.pallas_call(
        kernel,
        out_shape=(
            jax.ShapeDtypeStruct((rows, CHANNELS), BF16),
            jax.ShapeDtypeStruct((rows, CHANNELS), BF16),
            jax.ShapeDtypeStruct(weight_shape, F32),
            jax.ShapeDtypeStruct(weight_shape, F32),
        ),
        in_specs=[any_spec] * 7,
        out_specs=(any_spec,) * 4,
        scratch_shapes=[
            cells, cells,
            pltpu.VMEM(weight_shape, BF16), pltpu.VMEM(weight_shape, BF16),
            pltpu.VMEM((8, side, side), BF16),
            pltpu.VMEM((rows, rows), BF16), pltpu.VMEM((rows, rows), BF16),
            pairs, pairs, blocks, blocks, blocks, blocks, pairs, pairs,
            pltpu.VMEM((CHANNELS, CHANNELS), BF16), pltpu.VMEM((CHANNELS, CHANNELS), BF16),
            pltpu.VMEM((2, HALF, HALF), F32),
            lines, lines, lines, lines,
            pltpu.VMEM((LINES, CHANNELS), F32),
            pltpu.VMEM((OWN, side, HALF), BF16),
            pltpu.VMEM((CHANNELS, CHANNELS), F32),
            pltpu.VMEM((4, WIDTH, HALF), BF16),
            pltpu.VMEM((8, 48, HALF), BF16),
            pltpu.VMEM((TILES, 16, 128), BF16),
            pltpu.VMEM((dp_count, 16, 128), BF16),
            pltpu.VMEM((TILES, 16, 128), BF16),
            pltpu.VMEM((LON, TILES, 16, 128), BF16),
            pltpu.VMEM((WIDTH, HALF), F32),
            pltpu.VMEM(weight_shape, F32), pltpu.VMEM(weight_shape, F32),
            dma((8,)), dma((4,)), dma((4,)), dma((4, LON)), dma((4, LON)),
            dma((8,)), dma((8,)), dma((TILES,)), dma((dp_count,)),
            dma((dp_count,)), dma((TILES,)), dma((LON,)), dma((LON,)),
        ],
        compiler_params=pltpu.CompilerParams(
            collective_id=0, has_side_effects=True, vmem_limit_bytes=48 << 20
        ),
    )(
        fields.reshape(rows, CHANNELS), cotangent.reshape(rows, CHANNELS),
        first_weight, second_weight, lon, lat_fwd, lat_inv,
    )
    shape = (1, ROWS, LAT, CHANNELS)
    return wave.reshape(shape), pull.reshape(shape), grad1, grad2


def solution(mesh):
    placed = (P("dp", "lon", None, None), P("dp", "lon", None, None), P(), P())
    return jax.shard_map(
        on_device, mesh=mesh, in_specs=placed, out_specs=placed, check_vma=False
    )
```

time: 651 us -> 86.2 us (0.13); the launches traced: 643 us -> 85.8 us
  waiting for transfers between devices: 458 us -> 0 us
  local copies, waits for them, and re-layouts: 88.8 us -> 9.42 us
  Pallas kernels: 0 us -> 75.8 us
  starting transfers between devices: 51.6 us -> 0 us
  other arithmetic: 17.4 us -> 0 us
  between operations: 15 us -> 0.65 us
  matrix products: 12.2 us -> 0 us
    psum x1 -> x0, waiting for transfers between devices: 451 us -> none  [on_device(): first_grad, second_grad = lax.psum((first_term, second_term), ('dp', 'lon'))]
    pallas_call x0 -> x1, Pallas kernels: none -> 75.8 us  [on_device(): pl.pallas_call(kernel, out_shape=(jax.ShapeDtypeStruct((rows, CHANNELS),...]
    all_to_all x8 -> x0, starting transfers between devices: 51.6 us -> none  [the longest x2 16.1 us: to_spectrum(): lax.all_to_all(grid_rows, 'lon', split_axis=2, concat_axis=0, tiled=True)]
    unnamed x90 -> x16, local copies, waits for them, and re-layouts: 52.7 us -> 9.42 us
    convert_element_type x12 -> x0, local copies, waits for them, and re-layouts: 18.8 us -> none  [the longest x2 4.05 us: on_device(): pull.astype(jnp.float32)]
    all_to_all x10 -> x0, local copies, waits for them, and re-layouts: 14.4 us -> none  [the longest x4 7.92 us: lines_to_modes(): lax.all_to_all(local_dft(all_lines), 'lon', split_axis=0, concat_axis=3,...]
    dot_general x14 -> x0, matrix products: 12.2 us -> none  [the longest x2 3.01 us: local_idft(): jnp.einsum('kphc,wkp->whc', all_modes, dft_basis, preferred_element_type=...]
    all_to_all x8 -> x0, waiting for transfers between devices: 6.97 us -> none  [the longest x2 4.04 us: to_spectrum(): lax.all_to_all(grid_rows, 'lon', split_axis=2, concat_axis=0, tiled=True)]
  transfers between devices with their start and end apart: 9 -> 0, of which waited for: 4 -> 0; matrix products, arithmetic and copies ran while one was open for 13% -> 0% of each run, Pallas kernels for 0% -> 0%
where the time goes in v1:
time: 86.2 us; the launch traced here: 85.8 us
  Pallas kernels  75.8 us (88%)
  local copies, waits for them, and re-layouts  9.42 us (11%)
    pallas_call x1, Pallas kernels, on_device(): pl.pallas_call(kernel, out_shape=(jax.ShapeDtypeStruct((rows, CHANNELS),...  75.8 us
    unnamed x16, local copies, waits for them, and re-layouts  9.42 us

profile of v1, /device:TPU:1, one launch (start us, length us, event | category | flops | bytes accessed | tf_op | source)
XLA Modules:
  0.0 85.8 jit_solution(4848274387018592435)
XLA Ops:
  0.6 0.0 copy-start
  0.6 1.1 %copy-done = bf16[1,8,48,768]{3,2,1,0:T(8,128)(2,1)S(1)} copy-done((bf16[1,8,48,768]{3,2,1,0:T(8,128)(2,1)S(1)}, bf16[1,8,48,768]{3,2,1,0:T(8,128)(2,1)}, u32[]{:S(2)}) %copy-start) | copy-done | bytes 589848
  1.7 0.0 copy-start.1
  1.7 1.1 %copy-done.1 = bf16[1,8,48,768]{3,2,1,0:T(8,128)(2,1)S(1)} copy-done((bf16[1,8,48,768]{3,2,1,0:T(8,128)(2,1)S(1)}, bf16[1,8,48,768]{3,2,1,0:T(8,128)(2,1)}, u32[]{:S(2)}) %copy-start.1) | copy-done | bytes 589848
  2.8 0.0 copy-start.2
  2.8 1.0 %copy-done.2 = bf16[2,8,96,96]{3,2,1,0:T(8,128)(2,1)S(1)} copy-done((bf16[2,8,96,96]{3,2,1,0:T(8,128)(2,1)S(1)}, bf16[2,8,96,96]{3,2,1,0:T(8,128)(2,1)}, u32[]{:S(2)}) %copy-start.2) | copy-done | bytes 294936
  3.8 0.0 copy-start.3
  3.8 1.0 %copy-done.3 = bf16[2,8,96,96]{3,2,1,0:T(8,128)(2,1)S(1)} copy-done((bf16[2,8,96,96]{3,2,1,0:T(8,128)(2,1)S(1)}, bf16[2,8,96,96]{3,2,1,0:T(8,128)(2,1)}, u32[]{:S(2)}) %copy-start.3) | copy-done | bytes 294936
  4.8 0.0 copy-start.4
  4.8 1.0 %copy-done.4 = bf16[384,384]{1,0:T(8,128)(2,1)S(1)} copy-done((bf16[384,384]{1,0:T(8,128)(2,1)S(1)}, bf16[384,384]{1,0:T(8,128)(2,1)}, u32[]{:S(2)}) %copy-start.4) | copy-done | bytes 294936
  5.7 0.0 copy-start.5
  5.7 1.0 %copy-done.5 = bf16[384,384]{1,0:T(8,128)(2,1)S(1)} copy-done((bf16[384,384]{1,0:T(8,128)(2,1)S(1)}, bf16[384,384]{1,0:T(8,128)(2,1)}, u32[]{:S(2)}) %copy-start.5) | copy-done | bytes 294936
  6.7 75.8 %shard_map.102 = (bf16[384,768]{1,0:T(8,128)(2,1)S(1)}, bf16[384,768]{1,0:T(8,128)(2,1)S(1)}, f32[2,8,96,96]{3,2,1,0:T(8,128)S(1)}, f32[2,8,96,96]{3,2,1,0:T(8,128)S(1)}) custom-call(bf16[384,768]{1,0:T(8,128)(2,1)S(1)} %bitcast.4, bf16[384,768]{1,0:T(8,128)(2,1)S(1)} %bitcast.5, bf16[2,8,96,96]{3,2,1,0:T(8,128)(2,1)S(1)} %copy-done.2, ...), custom_call_target="tpu_custom_call" | custom-call | tf_op jit(solution)/shard_map/pallas_call | solution.py:533
  82.5 0.8 copy.15
  83.3 0.8 copy.16
  84.1 0.9 %copy.17 = f32[2,8,96,96]{3,2,1,0:T(8,128)} copy(f32[2,8,96,96]{3,2,1,0:T(8,128)S(1)} %get-tuple-element.18) | data formatting | bytes 1179648
  85.0 0.9 %copy.18 = f32[2,8,96,96]{3,2,1,0:T(8,128)} copy(f32[2,8,96,96]{3,2,1,0:T(8,128)S(1)} %get-tuple-element.19) | data formatting | bytes 1179648
Async XLA Ops:
  0.6 1.1 %copy-start = (bf16[1,8,48,768]{3,2,1,0:T(8,128)(2,1)S(1)}, bf16[1,8,48,768]{3,2,1,0:T(8,128)(2,1)}, u32[]{:S(2)}) copy-start(bf16[1,8,48,768]{3,2,1,0:T(8,128)(2,1)} %param.7) | copy-start | bytes 1769476
  1.7 1.1 %copy-start.1 = (bf16[1,8,48,768]{3,2,1,0:T(8,128)(2,1)S(1)}, bf16[1,8,48,768]{3,2,1,0:T(8,128)(2,1)}, u32[]{:S(2)}) copy-start(bf16[1,8,48,768]{3,2,1,0:T(8,128)(2,1)} %param.8) | copy-start | bytes 1769476
  2.8 1.0 %copy-start.2 = (bf16[2,8,96,96]{3,2,1,0:T(8,128)(2,1)S(1)}, bf16[2,8,96,96]{3,2,1,0:T(8,128)(2,1)}, u32[]{:S(2)}) copy-start(bf16[2,8,96,96]{3,2,1,0:T(8,128)(2,1)} %w1_hbm.1) | copy-start | bytes 884740
  3.8 1.0 %copy-start.3 = (bf16[2,8,96,96]{3,2,1,0:T(8,128)(2,1)S(1)}, bf16[2,8,96,96]{3,2,1,0:T(8,128)(2,1)}, u32[]{:S(2)}) copy-start(bf16[2,8,96,96]{3,2,1,0:T(8,128)(2,1)} %w2_hbm.1) | copy-start | bytes 884740
  4.8 1.0 %copy-start.4 = (bf16[384,384]{1,0:T(8,128)(2,1)S(1)}, bf16[384,384]{1,0:T(8,128)(2,1)}, u32[]{:S(2)}) copy-start(bf16[384,384]{1,0:T(8,128)(2,1)} %constant.8.clone.lati_hbm) | copy-start | bytes 884740
  5.7 1.0 %copy-start.5 = (bf16[384,384]{1,0:T(8,128)(2,1)S(1)}, bf16[384,384]{1,0:T(8,128)(2,1)}, u32[]{:S(2)}) copy-start(bf16[384,384]{1,0:T(8,128)(2,1)} %constant.7.clone.latf_hbm) | copy-start | bytes 884740

commit v2 on v1

--- a/solution.py
+++ b/solution.py
@@ -176,7 +176,7 @@
     def start_all(make, stage, src, dst):
         @pl.loop(1, LON)
         def _(i):
-            make(stage, src, dst, i).start()
+            make(stage, src, dst, LON - i).start()
 
     def arrived(stage, buf):
         @pl.loop(1, LON)
@@ -269,9 +269,6 @@
         lanes = slice(HALF * part, HALF * part + HALF)
         store_mixed(matmul(act[...], wide2[:, lanes]).astype(BF16), part)
     lon_inverse(3, back_x)
-    start_all(to_cells, 2, back_x, home_x)
-    keep_x = keep_back(back_x, home_x, 2)
-    keep_x.start()
 
     def outer(left, right, n):
         for m in range(6):
@@ -304,47 +301,53 @@
     def share(k):
         return grads.at[k // 2, pl.ds(pl.multiple_of(lax.rem(k, 2) * 48, 16), 48), :]
 
-    @pl.loop(1, 8)
-    def _(i):
+    def to_owner(i):
         k = lax.rem(e + i, 8)
-        pltpu.make_async_remote_copy(
+        return pltpu.make_async_remote_copy(
             src_ref=share(k),
             dst_ref=part1.at[e],
             send_sem=sum_out.at[i],
             recv_sem=sum_in.at[e],
             device_id=(dp, device_of(k, u)),
             device_id_type=MESH,
-        ).start()
+        )
+
+    def send_shares():
+        @pl.loop(1, 8)
+        def _(i):
+            to_owner(i).start()
+
+    send_shares()
 
     for part in range(2):
         rows = slice(HALF * part, HALF * part + HALF)
         store_mixed(contract(pre[...], wide1[rows, :], 1).astype(BF16), part)
     lon_inverse(2, back_y)
-    start_all(to_cells, 3, back_y, home_y)
-    keep_y = keep_back(back_y, home_y, 3)
-    keep_y.start()
-
-    part1[e] = share(e)[...]
-
-    @pl.loop(1, 8)
-    def _(i):
-        k = lax.rem(e + i, 8)
-        pltpu.make_async_remote_copy(
-            src_ref=part1.at[k],
-            dst_ref=part1.at[k],
-            send_sem=sum_out.at[i],
-            recv_sem=sum_in.at[k],
-            device_id=(dp, device_of(k, u)),
-            device_id_type=MESH,
-        ).wait_recv()
-
-    total = part1[0].astype(F32)
-    for k in range(1, 8):
-        total = total + part1[k].astype(F32)
-    total = total.astype(BF16)
-    for t in range(TILES):
-        a, b = t // 3, t % 3
-        own1[t] = total[16 * a : 16 * a + 16, 128 * b : 128 * b + 128]
+
+    def sum_shares():
+        part1[e] = share(e)[...]
+
+        @pl.loop(1, 8)
+        def _(i):
+            k = lax.rem(e + i, 8)
+            pltpu.make_async_remote_copy(
+                src_ref=part1.at[k],
+                dst_ref=part1.at[k],
+                send_sem=sum_out.at[i],
+                recv_sem=sum_in.at[k],
+                device_id=(dp, device_of(k, u)),
+                device_id_type=MESH,
+            ).wait_recv()
+
+        total = part1[0].astype(F32)
+        for k in range(1, 8):
+            total = total + part1[k].astype(F32)
+        total = total.astype(BF16)
+        for t in range(TILES):
+            a, b = t // 3, t % 3
+            own1[t] = total[16 * a : 16 * a + 16, 128 * b : 128 * b + 128]
+
+    sum_shares()
 
     def reducer(t):
         return (dp_count * t) // TILES
@@ -359,11 +362,20 @@
             device_id_type=MESH,
         )
 
-    @pl.loop(0, TILES)
-    def _(t):
-        @pl.when(dp != reducer(t))
-        def _():
-            to_reducer(t).start()
+    def send_tiles():
+        @pl.loop(0, TILES)
+        def _(t):
+            @pl.when(dp != reducer(t))
+            def _():
+                to_reducer(t).start()
+
+    send_tiles()
+    start_all(to_cells, 2, back_x, home_x)
+    keep_x = keep_back(back_x, home_x, 2)
+    keep_x.start()
+    start_all(to_cells, 3, back_y, home_y)
+    keep_y = keep_back(back_y, home_y, 3)
+    keep_y.start()
 
     def finish_cells(rows, home, out, n):
         for c in range(3):
@@ -373,10 +385,6 @@
             rows[:, lanes] = got.astype(BF16)
         return pltpu.make_async_copy(rows, out, store_sem.at[n])
 
-    keep_x.wait()
-    arrived(2, home_x)
-    store_x = finish_cells(xv, home_x, outx_hbm, 0)
-    store_x.start()
 
     mine = ((TILES * dp) + TILES - 1) // dp_count
     reduces = reducer(mine) == dp
@@ -416,6 +424,16 @@
         @pl.loop(1, dp_count)
         def _(i):
             to_all(i).start()
+
+    keep_x.wait()
+    arrived(2, home_x)
+    store_x = finish_cells(xv, home_x, outx_hbm, 0)
+    store_x.start()
+
+    keep_y.wait()
+    arrived(3, home_y)
+    store_y = finish_cells(yv, home_y, outy_hbm, 1)
+    store_y.start()
 
     @pl.loop(0, TILES)
     def _(t):
@@ -430,48 +448,85 @@
                 device_id_type=MESH,
             ).wait_recv()
 
-    def to_group(i):
+    twin = me + 1 - 2 * lax.rem(me, 2)
+
+    def to_chips(i):
         return pltpu.make_async_remote_copy(
             src_ref=own3,
             dst_ref=final.at[me],
             send_sem=gather_out.at[i],
             recv_sem=gather_in.at[me],
-            device_id=(dp, lax.rem(me + i, LON)),
-            device_id_type=MESH,
-        )
-
-    @pl.loop(1, LON)
-    def _(i):
-        to_group(i).start()
-
-    final[me] = own3[...]
-
-    keep_y.wait()
-    arrived(3, home_y)
-    store_y = finish_cells(yv, home_y, outy_hbm, 1)
-    store_y.start()
-
-    @pl.loop(1, LON)
-    def _(i):
-        s = lax.rem(me + i, LON)
-        pltpu.make_async_remote_copy(
+            device_id=(dp, lax.rem(me + 2 * i, LON)),
+            device_id_type=MESH,
+        )
+
+    def to_twin(i):
+        s = lax.rem(me + 2 * i, LON)
+        return pltpu.make_async_remote_copy(
             src_ref=final.at[s],
             dst_ref=final.at[s],
-            send_sem=gather_out.at[i],
+            send_sem=gather_out.at[8 + i],
             recv_sem=gather_in.at[s],
-            device_id=(dp, s),
-            device_id_type=MESH,
-        ).wait_recv()
-
-    for q in range(4):
-        out = (grad1, grad2)[q // 2]
-        for v in range(2):
-            for t in range(2 * TILES):
-                a, b = t // 3, t % 3
-                tile = final[4 * q + 2 * v + a // 3, 3 * (a % 3) + b]
-                strip[16 * a : 16 * a + 16, 128 * b : 128 * b + 128] = tile.astype(F32)
-            for g in range(4):
-                out[q % 2, 4 * v + g] = strip[:, WIDTH * g : WIDTH * g + WIDTH]
+            device_id=(dp, twin),
+            device_id_type=MESH,
+        )
+
+    def from_peer(s, sender):
+        return pltpu.make_async_remote_copy(
+            src_ref=final.at[s],
+            dst_ref=final.at[s],
+            send_sem=gather_out.at[0],
+            recv_sem=gather_in.at[s],
+            device_id=(dp, sender),
+            device_id_type=MESH,
+        )
+
+    def gather_start():
+        @pl.loop(1, 8)
+        def _(i):
+            to_chips(8 - i).start()
+
+        final[me] = own3[...]
+        to_twin(0).start()
+
+    def gather_forward():
+        @pl.loop(1, 8)
+        def _(i):
+            s = lax.rem(me + 2 * i, LON)
+            from_peer(s, s).wait_recv()
+            to_twin(i).start()
+
+    def gather_wait():
+        @pl.loop(0, 8)
+        def _(i):
+            from_peer(lax.rem(twin + 2 * i, LON), twin).wait_recv()
+
+    def gather_sent():
+        @pl.loop(1, 8)
+        def _(i):
+            to_chips(i).wait_send()
+            to_twin(i).wait_send()
+
+        to_twin(0).wait_send()
+
+    gather_start()
+
+    gather_forward()
+
+    gather_wait()
+
+    def unpack():
+        for q in range(4):
+            out = (grad1, grad2)[q // 2]
+            for v in range(2):
+                for t in range(2 * TILES):
+                    a, b = t // 3, t % 3
+                    tile = final[4 * q + 2 * v + a // 3, 3 * (a % 3) + b]
+                    strip[16 * a : 16 * a + 16, 128 * b : 128 * b + 128] = tile.astype(F32)
+                for g in range(4):
+                    out[q % 2, 4 * v + g] = strip[:, WIDTH * g : WIDTH * g + WIDTH]
+
+    unpack()
 
     stores = [
         pltpu.make_async_copy(grad1, grad1_hbm, store_sem.at[2]),
@@ -486,19 +541,14 @@
         to_mixer(1, send_y, recv_y, i).wait_send()
         to_cells(2, back_x, home_x, i).wait_send()
         to_cells(3, back_y, home_y, i).wait_send()
-        to_group(i).wait_send()
-
-    @pl.loop(1, 8)
-    def _(i):
-        k = lax.rem(e + i, 8)
-        pltpu.make_async_remote_copy(
-            src_ref=share(k),
-            dst_ref=part1.at[e],
-            send_sem=sum_out.at[i],
-            recv_sem=sum_in.at[e],
-            device_id=(dp, device_of(k, u)),
-            device_id_type=MESH,
-        ).wait_send()
+
+    def shares_sent():
+        @pl.loop(1, 8)
+        def _(i):
+            to_owner(i).wait_send()
+
+    shares_sent()
+    gather_sent()
 
     @pl.loop(0, TILES)
     def _(t):
@@ -565,7 +615,7 @@
             dma((dp_count,)), dma((TILES,)), dma((LON,)), dma((LON,)),
         ],
         compiler_params=pltpu.CompilerParams(
-            collective_id=0, has_side_effects=True, vmem_limit_bytes=48 << 20
+            collective_id=0, has_side_effects=True, vmem_limit_bytes=63 << 20
         ),
     )(
         fields.reshape(rows, CHANNELS), cotangent.reshape(rows, CHANNELS),

time: 86.2 us -> 76.4 us (0.89)
  Pallas kernels: 75.8 us -> 69.9 us
  local copies, waits for them, and re-layouts: 9.42 us -> 5.62 us
    pallas_call x1, Pallas kernels: 75.8 us -> 69.9 us  [on_device(): pl.pallas_call(kernel, out_shape=(jax.ShapeDtypeStruct((rows, CHANNELS),...]
    unnamed x16 -> x10, local copies, waits for them, and re-layouts: 9.42 us -> 5.62 us
where the time goes in v2:
time: 76.4 us; the launch traced here: 76.2 us
  Pallas kernels  69.9 us (91%)
  local copies, waits for them, and re-layouts  5.62 us (7%)
    pallas_call x1, Pallas kernels, on_device(): pl.pallas_call(kernel, out_shape=(jax.ShapeDtypeStruct((rows, CHANNELS),...  69.9 us
    unnamed x10, local copies, waits for them, and re-layouts  5.62 us

profile of v2, /device:TPU:1, one launch (start us, length us, event | category | flops | bytes accessed | tf_op | source)
XLA Modules:
  0.0 76.2 jit_solution(4218393985089633419)
XLA Ops:
  0.6 69.9 %shard_map.102 = (bf16[384,768]{1,0:T(8,128)(2,1)}, bf16[384,768]{1,0:T(8,128)(2,1)}, f32[2,8,96,96]{3,2,1,0:T(8,128)}, f32[2,8,96,96]{3,2,1,0:T(8,128)}) custom-call(bf16[384,768]{1,0:T(8,128)(2,1)} %bitcast.4, bf16[384,768]{1,0:T(8,128)(2,1)} %bitcast.5, bf16[2,8,96,96]{3,2,1,0:T(8,128)(2,1)} %w1_hbm.1, bf16[2,8,96,96]{3,2,1,0:T(8,128)(2,1)} %w2_hbm.1, ...), custom_call_target="tpu_custom_call" | custom-call | tf_op jit(solution)/shard_map/pallas_call | solution.py:583
  70.6 0.0 copy-start.2
  70.6 2.0 %copy.15 = bf16[1,8,48,768]{3,2,1,0:T(8,128)(2,1)} copy(bf16[1,8,48,768]{3,2,1,0:T(8,128)(2,1)} %bitcast.7) | data formatting | bytes 1179648
  72.6 0.0 copy-done.2
  72.6 0.0 copy-start.1
  72.6 0.8 %copy.16 = bf16[1,8,48,768]{3,2,1,0:T(8,128)(2,1)} copy(bf16[1,8,48,768]{3,2,1,0:T(8,128)(2,1)S(1)} %bitcast.6) | data formatting | bytes 1179648
  73.4 0.5 copy-done.1
  73.9 0.0 copy-start
  73.9 0.9 %copy.17 = f32[2,8,96,96]{3,2,1,0:T(8,128)} copy(f32[2,8,96,96]{3,2,1,0:T(8,128)S(1)} %copy-done.1) | data formatting | bytes 1179648
  74.8 0.5 copy-done
  75.3 0.9 %copy.18 = f32[2,8,96,96]{3,2,1,0:T(8,128)} copy(f32[2,8,96,96]{3,2,1,0:T(8,128)S(1)} %copy-done) | data formatting | bytes 1179648
Async XLA Ops:
  70.6 2.0 %copy-start.2 = (bf16[384,768]{1,0:T(8,128)(2,1)S(1)}, bf16[384,768]{1,0:T(8,128)(2,1)}, u32[]{:S(2)}) copy-start(bf16[384,768]{1,0:T(8,128)(2,1)} %get-tuple-element.9) | copy-start | bytes 1769476
  72.6 1.3 %copy-start.1 = (f32[2,8,96,96]{3,2,1,0:T(8,128)S(1)}, f32[2,8,96,96]{3,2,1,0:T(8,128)}, u32[]{:S(2)}) copy-start(f32[2,8,96,96]{3,2,1,0:T(8,128)} %get-tuple-element.18) | copy-start | bytes 1769476
  73.9 1.4 %copy-start = (f32[2,8,96,96]{3,2,1,0:T(8,128)S(1)}, f32[2,8,96,96]{3,2,1,0:T(8,128)}, u32[]{:S(2)}) copy-start(f32[2,8,96,96]{3,2,1,0:T(8,128)} %get-tuple-element.19) | copy-start | bytes 1769476

commit v3 on v2

--- a/solution.py
+++ b/solution.py
@@ -83,24 +83,19 @@
     return jnp.dot(left, right, preferred_element_type=F32)
 
 
-def contract(left, right, axis):
-    return lax.dot_general(
-        left, right, (((axis,), (axis,)), ((), ())), preferred_element_type=F32
-    )
-
-
 def kernel(
     x_hbm, y_hbm, w1_hbm, w2_hbm, lon_hbm, latf_hbm, lati_hbm,
-    outx_hbm, outy_hbm, grad1_hbm, grad2_hbm,
+    outx_hbm, outy_hbm, grads_hbm,
     xv, yv, w1v, w2v, lonv, latf, lati,
     send_x, send_y, recv_x, recv_y, back_x, back_y, home_x, home_y,
-    wide1, wide2, place, spec, dual, act, pre, slope, mixed,
-    square, grads, part1, own1, part2, own3, final, strip, grad1, grad2,
+    wide1, wide2, turned1, turned2, place, spec, dual, act, pre, slope, mixed,
+    spec_t, act_t, grads, part1, own1, part2, own3, final,
     load_sem, store_sem, self_sem, out_sem, in_sem,
-    sum_out, sum_in, dp_out, dp_in, cast_out, cast_in, gather_out, gather_in,
+    sum_out, sum_in, dp_out, dp_in, cast_out, cast_in, gather_out, gather_in, relay,
 ):
     dp_count = lax.axis_size("dp")
     me, dp = lax.axis_index("lon"), lax.axis_index("dp")
+    ring, z, side = dp_count // 2, dp // 2, lax.rem(dp, 2)
 
     def half_of(s):
         return lax.rem(s // 2, 2)
@@ -124,9 +119,6 @@
         pltpu.make_async_copy(lon_hbm.at[pl.ds(first, 4)], lonv.at[pl.ds(4, 4)], load_sem.at[6]),
         pltpu.make_async_copy(lati_hbm, lati, load_sem.at[7]),
     ]
-    for load in loads:
-        load.start()
-
     barrier = pltpu.get_barrier_semaphore()
 
     @pl.loop(1, LON)
@@ -135,11 +127,24 @@
             barrier, inc=1, device_id=(dp, lax.rem(me + i, LON)), device_id_type=MESH
         )
 
-    @pl.loop(1, dp_count)
-    def _(i):
-        pl.semaphore_signal(
-            barrier, inc=1, device_id=(lax.rem(dp + i, dp_count), me), device_id_type=MESH
-        )
+    def along(step):
+        return lax.rem(z + step + ring, ring) * 2 + side
+
+    turn = 1 - 2 * side
+    for other in (along(1), along(-1), dp + turn, along(1) + turn, along(-1) + turn):
+        pl.semaphore_signal(barrier, inc=1, device_id=(other, me), device_id_type=MESH)
+
+    for load in loads:
+        load.start()
+
+    def announce(r):
+        for step in (2**r, -(2**r)):
+            pl.semaphore_signal(
+                relay.at[r], inc=1, device_id=(along(step), me), device_id_type=MESH
+            )
+
+    def heard(r):
+        pl.semaphore_wait(relay.at[r], 2)
 
     def lat_forward(rows, out):
         for n in range(3):
@@ -204,7 +209,7 @@
     loads[0].wait()
     loads[1].wait()
     lat_forward(xv, send_x)
-    pl.semaphore_wait(barrier, LON - 1 + dp_count - 1)
+    pl.semaphore_wait(barrier, LON - 1 + 5)
     start_all(to_mixer, 0, send_x, recv_x)
     keep_x = keep_forward(send_x, recv_x, 0)
     keep_x.start()
@@ -213,8 +218,9 @@
     start_all(to_mixer, 1, send_y, recv_y)
     keep_y = keep_forward(send_y, recv_y, 1)
     keep_y.start()
-
-    def widen(weight, wide):
+    announce(0)
+
+    def widen(weight, wide, turned):
         for p in range(2):
             for g in range(4):
                 own = slice(WIDTH * g, WIDTH * g + WIDTH)
@@ -224,12 +230,19 @@
         wide[HALF:, HALF:] = real
         wide[:HALF, HALF:] = imag
         wide[HALF:, :HALF] = -imag
+        real, imag = place[0].T.astype(BF16), place[1].T.astype(BF16)
+        turned[:HALF, :HALF] = real
+        turned[HALF:, HALF:] = real
+        turned[:HALF, HALF:] = -imag
+        turned[HALF:, :HALF] = imag
 
     place[...] = jnp.zeros_like(place)
     for load in loads[3:]:
         load.wait()
-    widen(w1v, wide1)
-    widen(w2v, wide2)
+    widen(w1v, wide1, turned1)
+    widen(w2v, wide2, turned2)
+    heard(0)
+    announce(1)
 
     def lon_forward(buf, kind, out):
         for p in range(OWN):
@@ -270,33 +283,36 @@
         store_mixed(matmul(act[...], wide2[:, lanes]).astype(BF16), part)
     lon_inverse(3, back_x)
 
-    def outer(left, right, n):
-        for m in range(6):
-            lanes = slice(128 * m, 128 * m + 128)
-            square[lanes, :] = contract(left[:, lanes], right[...], 0)
+    heard(1)
+    announce(2)
+
+    spec_t[...] = spec[...].T
+    act_t[...] = act[...].T
+
+    def outer(left_t, right, n):
         lane = lax.broadcasted_iota(jnp.int32, (WIDTH, 128), 1)
         for b in range(3):
             low = slice(128 * b, 128 * b + 128)
             high = slice(HALF + 128 * b, HALF + 128 * b + 128)
-            sums, gaps = [], []
-            for g in (b, b + 1):
-                top = slice(WIDTH * g, WIDTH * g + WIDTH)
-                bottom = slice(HALF + WIDTH * g, HALF + WIDTH * g + WIDTH)
-                sums.append(square[top, low] + square[bottom, high])
-                gaps.append(square[top, high] - square[bottom, low])
+            columns = jnp.concatenate([right[:, low], right[:, high]], axis=1)
+            span = 2 * WIDTH
+            top = matmul(left_t[WIDTH * b : WIDTH * b + span, :], columns)
+            bottom = matmul(left_t[HALF + WIDTH * b : HALF + WIDTH * b + span, :], columns)
+            sums = top[:, :128] + bottom[:, 128:]
+            gaps = top[:, 128:] - bottom[:, :128]
             mine = lane < WIDTH - 32 * b
-            grads[n, :, low] = jnp.where(mine, sums[0], sums[1]).astype(BF16)
-            grads[n + 1, :, low] = jnp.where(mine, gaps[0], gaps[1]).astype(BF16)
+            grads[n, :, low] = jnp.where(mine, sums[:WIDTH], sums[WIDTH:]).astype(BF16)
+            grads[n + 1, :, low] = jnp.where(mine, gaps[:WIDTH], gaps[WIDTH:]).astype(BF16)
 
     keep_y.wait()
     arrived(1, recv_y)
     lon_forward(recv_y, 1, dual)
     for part in range(2):
         rows = slice(HALF * part, HALF * part + HALF)
-        back = contract(dual[...], wide2[rows, :], 1)
+        back = matmul(dual[...], turned2[:, rows])
         pre[:, rows] = (back * slope[:, rows]).astype(BF16)
-    outer(spec, pre, 0)
-    outer(act, dual, 2)
+    outer(spec_t, pre, 0)
+    outer(act_t, dual, 2)
 
     def share(k):
         return grads.at[k // 2, pl.ds(pl.multiple_of(lax.rem(k, 2) * 48, 16), 48), :]
@@ -321,7 +337,7 @@
 
     for part in range(2):
         rows = slice(HALF * part, HALF * part + HALF)
-        store_mixed(contract(pre[...], wide1[rows, :], 1).astype(BF16), part)
+        store_mixed(matmul(pre[...], turned1[:, rows]).astype(BF16), part)
     lon_inverse(2, back_y)
 
     def sum_shares():
@@ -348,26 +364,39 @@
             own1[t] = total[16 * a : 16 * a + 16, 128 * b : 128 * b + 128]
 
     sum_shares()
-
-    def reducer(t):
-        return (dp_count * t) // TILES
-
-    def to_reducer(t):
+    heard(2)
+
+    def place_of(t):
+        return (16 * t) // TILES
+
+    def reducer(t, h):
+        return lax.rem(place_of(t) + 8 * h, 16) * 2 + lax.rem(t, 2)
+
+    def near_reducer(t):
+        far = lax.rem(z - place_of(t) + 20, 16) // 8
+        return reducer(t, far)
+
+    def to_reducer(t, h):
         return pltpu.make_async_remote_copy(
             src_ref=own1.at[t],
             dst_ref=part2.at[dp],
-            send_sem=dp_out.at[t],
+            send_sem=dp_out.at[2 * t + h],
             recv_sem=dp_in.at[dp],
-            device_id=(reducer(t), me),
-            device_id_type=MESH,
-        )
+            device_id=(reducer(t, h), me),
+            device_id_type=MESH,
+        )
+
+    def each_reducer(act_on):
+        @pl.loop(0, 2 * TILES)
+        def _(n):
+            t, h = n // 2, lax.rem(n, 2)
+
+            @pl.when(dp != reducer(t, h))
+            def _():
+                act_on(to_reducer(t, h))
 
     def send_tiles():
-        @pl.loop(0, TILES)
-        def _(t):
-            @pl.when(dp != reducer(t))
-            def _():
-                to_reducer(t).start()
+        each_reducer(lambda copy: copy.start())
 
     send_tiles()
     start_all(to_cells, 2, back_x, home_x)
@@ -386,11 +415,19 @@
         return pltpu.make_async_copy(rows, out, store_sem.at[n])
 
 
-    mine = ((TILES * dp) + TILES - 1) // dp_count
-    reduces = reducer(mine) == dp
+    spot = lax.rem(z, 8)
+    mine = jnp.where(
+        lax.rem(spot, 2) == 1,
+        (spot + 1) // 2,
+        jnp.where(spot == 0, 5 * side, 5 + spot // 2),
+    )
+    reduces = lax.rem(mine, 2) == side
+
+    def neighbour(i):
+        return lax.rem(z + i // 2 + 12, 16) * 2 + lax.rem(i, 2)
 
     def to_all(i):
-        d = lax.rem(dp + i, dp_count)
+        d = neighbour(i)
         return pltpu.make_async_remote_copy(
             src_ref=own3.at[mine],
             dst_ref=own3.at[mine],
@@ -421,9 +458,11 @@
             whole = whole + part2[d].astype(F32)
         own3[mine] = (whole * (1.0 / SAMPLES)).astype(BF16)
 
-        @pl.loop(1, dp_count)
-        def _(i):
-            to_all(i).start()
+        @pl.loop(0, 16)
+        def _(i):
+            @pl.when(neighbour(i) != dp)
+            def _():
+                to_all(i).start()
 
     keep_x.wait()
     arrived(2, home_x)
@@ -437,14 +476,14 @@
 
     @pl.loop(0, TILES)
     def _(t):
-        @pl.when(dp != reducer(t))
+        @pl.when(dp != near_reducer(t))
         def _():
             pltpu.make_async_remote_copy(
                 src_ref=own3.at[t],
                 dst_ref=own3.at[t],
                 send_sem=cast_out.at[0],
                 recv_sem=cast_in.at[t],
-                device_id=(reducer(t), me),
+                device_id=(near_reducer(t), me),
                 device_id_type=MESH,
             ).wait_recv()
 
@@ -515,25 +554,8 @@
 
     gather_wait()
 
-    def unpack():
-        for q in range(4):
-            out = (grad1, grad2)[q // 2]
-            for v in range(2):
-                for t in range(2 * TILES):
-                    a, b = t // 3, t % 3
-                    tile = final[4 * q + 2 * v + a // 3, 3 * (a % 3) + b]
-                    strip[16 * a : 16 * a + 16, 128 * b : 128 * b + 128] = tile.astype(F32)
-                for g in range(4):
-                    out[q % 2, 4 * v + g] = strip[:, WIDTH * g : WIDTH * g + WIDTH]
-
-    unpack()
-
-    stores = [
-        pltpu.make_async_copy(grad1, grad1_hbm, store_sem.at[2]),
-        pltpu.make_async_copy(grad2, grad2_hbm, store_sem.at[3]),
-    ]
-    for store in stores:
-        store.start()
+    store_final = pltpu.make_async_copy(final, grads_hbm, store_sem.at[2])
+    store_final.start()
 
     @pl.loop(1, LON)
     def _(i):
@@ -550,19 +572,53 @@
     shares_sent()
     gather_sent()
 
-    @pl.loop(0, TILES)
-    def _(t):
-        @pl.when(dp != reducer(t))
-        def _():
-            to_reducer(t).wait_send()
+    each_reducer(lambda copy: copy.wait_send())
 
     @pl.when(reduces)
     def _():
-        @pl.loop(1, dp_count)
-        def _(i):
-            to_all(i).wait_send()
-
-    for store in [store_x, store_y, *stores]:
+        @pl.loop(0, 16)
+        def _(i):
+            @pl.when(neighbour(i) != dp)
+            def _():
+                to_all(i).wait_send()
+
+    for store in [store_x, store_y, store_final]:
+        store.wait()
+
+
+def deliver(
+    x_hbm, y_hbm, grads_hbm, outx_hbm, outy_hbm, grad1_hbm, grad2_hbm,
+    xv, yv, final, strip, grad1, grad2, in_sem, out_sem,
+):
+    loads = [
+        pltpu.make_async_copy(grads_hbm, final, in_sem.at[0]),
+        pltpu.make_async_copy(x_hbm, xv, in_sem.at[1]),
+        pltpu.make_async_copy(y_hbm, yv, in_sem.at[2]),
+    ]
+    for load in loads:
+        load.start()
+    stores = [
+        pltpu.make_async_copy(xv, outx_hbm, out_sem.at[0]),
+        pltpu.make_async_copy(yv, outy_hbm, out_sem.at[1]),
+        pltpu.make_async_copy(grad1, grad1_hbm, out_sem.at[2]),
+        pltpu.make_async_copy(grad2, grad2_hbm, out_sem.at[3]),
+    ]
+    loads[0].wait()
+    for q in range(4):
+        out = (grad1, grad2)[q // 2]
+        for v in range(2):
+            for t in range(2 * TILES):
+                a, b = t // 3, t % 3
+                tile = final[4 * q + 2 * v + a // 3, 3 * (a % 3) + b]
+                strip[16 * a : 16 * a + 16, 128 * b : 128 * b + 128] = tile.astype(F32)
+            for g in range(4):
+                out[q % 2, 4 * v + g] = strip[:, WIDTH * g : WIDTH * g + WIDTH]
+        if q < 2:
+            loads[1 + q].wait()
+            stores[q].start()
+        if q % 2 == 1:
+            stores[2 + q // 2].start()
+    for store in stores:
         store.wait()
 
 
@@ -579,40 +635,39 @@
     pairs = pltpu.VMEM((PAIRS, TILE, CHANNELS), BF16)
     lines = pltpu.VMEM((LINES, CHANNELS), BF16)
     blocks = pltpu.VMEM((OWN, LON, TILE, HALF), BF16)
+    wide = pltpu.VMEM((CHANNELS, CHANNELS), BF16)
+    turned = pltpu.VMEM((CHANNELS, LINES), BF16)
     side = 4 * MODES
-    wave, pull, grad1, grad2 = pl.pallas_call(
+    cell_shape = jax.ShapeDtypeStruct((rows, CHANNELS), BF16)
+    grad_shape = jax.ShapeDtypeStruct(weight_shape, F32)
+    final_shape = (LON, TILES, 16, 128)
+    results = pl.pallas_call(
         kernel,
-        out_shape=(
-            jax.ShapeDtypeStruct((rows, CHANNELS), BF16),
-            jax.ShapeDtypeStruct((rows, CHANNELS), BF16),
-            jax.ShapeDtypeStruct(weight_shape, F32),
-            jax.ShapeDtypeStruct(weight_shape, F32),
-        ),
+        out_shape=(cell_shape, cell_shape, jax.ShapeDtypeStruct(final_shape, BF16)),
         in_specs=[any_spec] * 7,
-        out_specs=(any_spec,) * 4,
+        out_specs=(any_spec,) * 3,
         scratch_shapes=[
             cells, cells,
             pltpu.VMEM(weight_shape, BF16), pltpu.VMEM(weight_shape, BF16),
             pltpu.VMEM((8, side, side), BF16),
             pltpu.VMEM((rows, rows), BF16), pltpu.VMEM((rows, rows), BF16),
             pairs, pairs, blocks, blocks, blocks, blocks, pairs, pairs,
-            pltpu.VMEM((CHANNELS, CHANNELS), BF16), pltpu.VMEM((CHANNELS, CHANNELS), BF16),
+            wide, wide, wide, wide,
             pltpu.VMEM((2, HALF, HALF), F32),
             lines, lines, lines, lines,
             pltpu.VMEM((LINES, CHANNELS), F32),
             pltpu.VMEM((OWN, side, HALF), BF16),
-            pltpu.VMEM((CHANNELS, CHANNELS), F32),
+            turned, turned,
             pltpu.VMEM((4, WIDTH, HALF), BF16),
             pltpu.VMEM((8, 48, HALF), BF16),
             pltpu.VMEM((TILES, 16, 128), BF16),
             pltpu.VMEM((dp_count, 16, 128), BF16),
             pltpu.VMEM((TILES, 16, 128), BF16),
             pltpu.VMEM((LON, TILES, 16, 128), BF16),
-            pltpu.VMEM((WIDTH, HALF), F32),
-            pltpu.VMEM(weight_shape, F32), pltpu.VMEM(weight_shape, F32),
-            dma((8,)), dma((4,)), dma((4,)), dma((4, LON)), dma((4, LON)),
-            dma((8,)), dma((8,)), dma((TILES,)), dma((dp_count,)),
-            dma((dp_count,)), dma((TILES,)), dma((LON,)), dma((LON,)),
+            dma((8,)), dma((3,)), dma((4,)), dma((4, LON)), dma((4, LON)),
+            dma((8,)), dma((8,)), dma((2 * TILES,)), dma((dp_count,)),
+            dma((16,)), dma((TILES,)), dma((LON,)), dma((LON,)),
+            pltpu.SemaphoreType.REGULAR((3,)),
         ],
         compiler_params=pltpu.CompilerParams(
             collective_id=0, has_side_effects=True, vmem_limit_bytes=63 << 20
@@ -621,6 +676,18 @@
         fields.reshape(rows, CHANNELS), cotangent.reshape(rows, CHANNELS),
         first_weight, second_weight, lon, lat_fwd, lat_inv,
     )
+    wave, pull, grad1, grad2 = pl.pallas_call(
+        deliver,
+        out_shape=(cell_shape, cell_shape, grad_shape, grad_shape),
+        in_specs=[any_spec] * 3,
+        out_specs=(any_spec,) * 4,
+        scratch_shapes=[
+            cells, cells, pltpu.VMEM(final_shape, BF16), pltpu.VMEM((WIDTH, HALF), F32),
+            pltpu.VMEM(weight_shape, F32), pltpu.VMEM(weight_shape, F32),
+            dma((3,)), dma((4,)),
+        ],
+        compiler_params=pltpu.CompilerParams(vmem_limit_bytes=63 << 20),
+    )(*results)
     shape = (1, ROWS, LAT, CHANNELS)
     return wave.reshape(shape), pull.reshape(shape), grad1, grad2
 

time: 76.4 us -> 68.6 us (0.90)
  local copies, waits for them, and re-layouts: 5.62 us -> 0 us
  Pallas kernels: 69.9 us -> 67.8 us
    unnamed x10 -> x0, local copies, waits for them, and re-layouts: 5.62 us -> none
    pallas_call x1 -> x2, Pallas kernels: 69.9 us -> 67.8 us  [the longest x1 65 us: on_device(): pl.pallas_call(kernel, out_shape=(cell_shape, cell_shape, jax.ShapeDtypeS...]
where the time goes in v3:
time: 68.6 us; the launch traced here: 68.5 us
  Pallas kernels  67.8 us (99%)
    pallas_call x1, Pallas kernels, on_device(): pl.pallas_call(kernel, out_shape=(cell_shape, cell_shape, jax.ShapeDtypeS...  65 us
    pallas_call x1, Pallas kernels, on_device(): pl.pallas_call(deliver, out_shape=(cell_shape, cell_shape, grad_shape, gr...  2.83 us

profile of v3, /device:TPU:1, one launch (start us, length us, event | category | flops | bytes accessed | tf_op | source)
XLA Modules:
  0.0 68.5 jit_solution(4543343479800086944)
XLA Ops:
  0.6 65.0 %shard_map.102 = (bf16[384,768]{1,0:T(8,128)(2,1)}, bf16[384,768]{1,0:T(8,128)(2,1)}, bf16[16,9,16,128]{3,2,1,0:T(8,128)(2,1)}) custom-call(bf16[384,768]{1,0:T(8,128)(2,1)} %bitcast.4, bf16[384,768]{1,0:T(8,128)(2,1)} %bitcast.5, bf16[2,8,96,96]{3,2,1,0:T(8,128)(2,1)} %w1_hbm.1, bf16[2,8,96,96]{3,2,1,0:T(8,128)(2,1)} %w2_hbm.1, ...), custom_call_target="tpu_custom_call" | custom-call | tf_op jit(solution)/shard_map/pallas_call | solution.py:644
  65.7 2.8 %shard_map.103 = (bf16[384,768]{1,0:T(8,128)(2,1)}, bf16[384,768]{1,0:T(8,128)(2,1)}, f32[2,8,96,96]{3,2,1,0:T(8,128)}, f32[2,8,96,96]{3,2,1,0:T(8,128)}) custom-call(bf16[384,768]{1,0:T(8,128)(2,1)} %get-tuple-element.11.x_hbm, bf16[384,768]{1,0:T(8,128)(2,1)} %get-tuple-element.12.y_hbm, bf16[16,9,16,128]{3,2,1,0:T(8,128)(2,1)} %get-tuple-element.13.grads_hbm), custom_call_target="tpu_custom_call" | custom-call | tf_op jit(solution)/shard_map/pallas_call | solution.py:679

commit v4 on v3

--- a/solution.py
+++ b/solution.py
@@ -304,36 +304,42 @@
             grads[n, :, low] = jnp.where(mine, sums[:WIDTH], sums[WIDTH:]).astype(BF16)
             grads[n + 1, :, low] = jnp.where(mine, gaps[:WIDTH], gaps[WIDTH:]).astype(BF16)
 
+    def share(k):
+        return grads.at[k // 2, pl.ds(pl.multiple_of(lax.rem(k, 2) * 48, 16), 48), :]
+
+    def to_owner(k):
+        return pltpu.make_async_remote_copy(
+            src_ref=share(k),
+            dst_ref=part1.at[e],
+            send_sem=sum_out.at[k],
+            recv_sem=sum_in.at[e],
+            device_id=(dp, device_of(k, u)),
+            device_id_type=MESH,
+        )
+
+    def each_owner(low, act_on):
+        @pl.loop(0, 4)
+        def _(i):
+            k = low + lax.rem(e + 2 + i, 4)
+
+            @pl.when(k != e)
+            def _():
+                act_on(to_owner(k))
+
+    def start(copy):
+        copy.start()
+
     keep_y.wait()
     arrived(1, recv_y)
     lon_forward(recv_y, 1, dual)
+    outer(act_t, dual, 2)
+    each_owner(4, start)
     for part in range(2):
         rows = slice(HALF * part, HALF * part + HALF)
         back = matmul(dual[...], turned2[:, rows])
         pre[:, rows] = (back * slope[:, rows]).astype(BF16)
     outer(spec_t, pre, 0)
-    outer(act_t, dual, 2)
-
-    def share(k):
-        return grads.at[k // 2, pl.ds(pl.multiple_of(lax.rem(k, 2) * 48, 16), 48), :]
-
-    def to_owner(i):
-        k = lax.rem(e + i, 8)
-        return pltpu.make_async_remote_copy(
-            src_ref=share(k),
-            dst_ref=part1.at[e],
-            send_sem=sum_out.at[i],
-            recv_sem=sum_in.at[e],
-            device_id=(dp, device_of(k, u)),
-            device_id_type=MESH,
-        )
-
-    def send_shares():
-        @pl.loop(1, 8)
-        def _(i):
-            to_owner(i).start()
-
-    send_shares()
+    each_owner(0, start)
 
     for part in range(2):
         rows = slice(HALF * part, HALF * part + HALF)
@@ -349,7 +355,7 @@
             pltpu.make_async_remote_copy(
                 src_ref=part1.at[k],
                 dst_ref=part1.at[k],
-                send_sem=sum_out.at[i],
+                send_sem=sum_out.at[k],
                 recv_sem=sum_in.at[k],
                 device_id=(dp, device_of(k, u)),
                 device_id_type=MESH,
@@ -405,6 +411,14 @@
     start_all(to_cells, 3, back_y, home_y)
     keep_y = keep_back(back_y, home_y, 3)
     keep_y.start()
+
+    @pl.loop(1, LON)
+    def _(i):
+        to_mixer(0, send_x, recv_x, i).wait_send()
+        to_mixer(1, send_y, recv_y, i).wait_send()
+
+    for low in (0, 4):
+        each_owner(low, lambda copy: copy.wait_send())
 
     def finish_cells(rows, home, out, n):
         for c in range(3):
@@ -550,27 +564,10 @@
 
     gather_start()
 
-    gather_forward()
-
-    gather_wait()
-
-    store_final = pltpu.make_async_copy(final, grads_hbm, store_sem.at[2])
-    store_final.start()
-
     @pl.loop(1, LON)
     def _(i):
-        to_mixer(0, send_x, recv_x, i).wait_send()
-        to_mixer(1, send_y, recv_y, i).wait_send()
         to_cells(2, back_x, home_x, i).wait_send()
         to_cells(3, back_y, home_y, i).wait_send()
-
-    def shares_sent():
-        @pl.loop(1, 8)
-        def _(i):
-            to_owner(i).wait_send()
-
-    shares_sent()
-    gather_sent()
 
     each_reducer(lambda copy: copy.wait_send())
 
@@ -582,6 +579,14 @@
             def _():
                 to_all(i).wait_send()
 
+    gather_forward()
+
+    gather_wait()
+
+    store_final = pltpu.make_async_copy(final, grads_hbm, store_sem.at[2])
+    store_final.start()
+
+    gather_sent()
     for store in [store_x, store_y, store_final]:
         store.wait()
 

time: 68.6 us -> 67.6 us (0.985)
  Pallas kernels: 67.8 us -> 66.8 us
    pallas_call x1, Pallas kernels: 65 us -> 64 us  [on_device(): pl.pallas_call(kernel, out_shape=(cell_shape, cell_shape, jax.ShapeDtypeS...]
where the time goes in v4:
time: 67.6 us; the launch traced here: 67.4 us
  Pallas kernels  66.8 us (99%)
    pallas_call x1, Pallas kernels, on_device(): pl.pallas_call(kernel, out_shape=(cell_shape, cell_shape, jax.ShapeDtypeS...  64 us
    pallas_call x1, Pallas kernels, on_device(): pl.pallas_call(deliver, out_shape=(cell_shape, cell_shape, grad_shape, gr...  2.83 us

profile of v4, /device:TPU:1, one launch (start us, length us, event | category | flops | bytes accessed | tf_op | source)
XLA Modules:
  0.0 67.4 jit_solution(16143034416427808610)
XLA Ops:
  0.6 64.0 %shard_map.102 = (bf16[384,768]{1,0:T(8,128)(2,1)}, bf16[384,768]{1,0:T(8,128)(2,1)}, bf16[16,9,16,128]{3,2,1,0:T(8,128)(2,1)}) custom-call(bf16[384,768]{1,0:T(8,128)(2,1)} %bitcast.4, bf16[384,768]{1,0:T(8,128)(2,1)} %bitcast.5, bf16[2,8,96,96]{3,2,1,0:T(8,128)(2,1)} %w1_hbm.1, bf16[2,8,96,96]{3,2,1,0:T(8,128)(2,1)} %w2_hbm.1, ...), custom_call_target="tpu_custom_call" | custom-call | tf_op jit(solution)/shard_map/pallas_call | solution.py:649
  64.6 2.8 %shard_map.103 = (bf16[384,768]{1,0:T(8,128)(2,1)}, bf16[384,768]{1,0:T(8,128)(2,1)}, f32[2,8,96,96]{3,2,1,0:T(8,128)}, f32[2,8,96,96]{3,2,1,0:T(8,128)}) custom-call(bf16[384,768]{1,0:T(8,128)(2,1)} %get-tuple-element.11.x_hbm, bf16[384,768]{1,0:T(8,128)(2,1)} %get-tuple-element.12.y_hbm, bf16[16,9,16,128]{3,2,1,0:T(8,128)(2,1)} %get-tuple-element.13.grads_hbm), custom_call_target="tpu_custom_call" | custom-call | tf_op jit(solution)/shard_map/pallas_call | solution.py:684

commit v5 on v4

--- a/solution.py
+++ b/solution.py
@@ -483,11 +483,6 @@
     store_x = finish_cells(xv, home_x, outx_hbm, 0)
     store_x.start()
 
-    keep_y.wait()
-    arrived(3, home_y)
-    store_y = finish_cells(yv, home_y, outy_hbm, 1)
-    store_y.start()
-
     @pl.loop(0, TILES)
     def _(t):
         @pl.when(dp != near_reducer(t))
@@ -563,6 +558,11 @@
         to_twin(0).wait_send()
 
     gather_start()
+
+    keep_y.wait()
+    arrived(3, home_y)
+    store_y = finish_cells(yv, home_y, outy_hbm, 1)
+    store_y.start()
 
     @pl.loop(1, LON)
     def _(i):

time: 67.6 us -> 66.8 us (0.988)
  Pallas kernels: 66.8 us -> 66 us
    pallas_call x1, Pallas kernels: 64 us -> 63.2 us  [on_device(): pl.pallas_call(kernel, out_shape=(cell_shape, cell_shape, jax.ShapeDtypeS...]
where the time goes in v5:
time: 66.8 us; the launch traced here: 66.7 us
  Pallas kernels  66 us (99%)
    pallas_call x1, Pallas kernels, on_device(): pl.pallas_call(kernel, out_shape=(cell_shape, cell_shape, jax.ShapeDtypeS...  63.2 us
    pallas_call x1, Pallas kernels, on_device(): pl.pallas_call(deliver, out_shape=(cell_shape, cell_shape, grad_shape, gr...  2.83 us

profile of v5, /device:TPU:1, one launch (start us, length us, event | category | flops | bytes accessed | tf_op | source)
XLA Modules:
  0.0 66.7 jit_solution(3017804430253244893)
XLA Ops:
  0.6 63.2 %shard_map.102 = (bf16[384,768]{1,0:T(8,128)(2,1)}, bf16[384,768]{1,0:T(8,128)(2,1)}, bf16[16,9,16,128]{3,2,1,0:T(8,128)(2,1)}) custom-call(bf16[384,768]{1,0:T(8,128)(2,1)} %bitcast.4, bf16[384,768]{1,0:T(8,128)(2,1)} %bitcast.5, bf16[2,8,96,96]{3,2,1,0:T(8,128)(2,1)} %w1_hbm.1, bf16[2,8,96,96]{3,2,1,0:T(8,128)(2,1)} %w2_hbm.1, ...), custom_call_target="tpu_custom_call" | custom-call | tf_op jit(solution)/shard_map/pallas_call | solution.py:649
  63.8 2.8 %shard_map.103 = (bf16[384,768]{1,0:T(8,128)(2,1)}, bf16[384,768]{1,0:T(8,128)(2,1)}, f32[2,8,96,96]{3,2,1,0:T(8,128)}, f32[2,8,96,96]{3,2,1,0:T(8,128)}) custom-call(bf16[384,768]{1,0:T(8,128)(2,1)} %get-tuple-element.11.x_hbm, bf16[384,768]{1,0:T(8,128)(2,1)} %get-tuple-element.12.y_hbm, bf16[16,9,16,128]{3,2,1,0:T(8,128)(2,1)} %get-tuple-element.13.grads_hbm), custom_call_target="tpu_custom_call" | custom-call | tf_op jit(solution)/shard_map/pallas_call | solution.py:684
